TPU v7x, 512 devices: a whole 4x4x16 slice. The times are simulated.
512 devices in a mesh: win: 8 (over y, core), frame: 64 (over z, x).
Axes of the slice: x: 4, y: 4, z: 16, core: 2. Of those that a mesh axis runs over, the one named last changes fastest.
Arguments:
- distances: float32 [32, 131072], P(None, 'frame'), may hold values from 0.05 to 9
- sample_ids: int32 [131072], P('frame'), may hold values from 0 to 4095, as said below
- lengths: int32 [64], replicated, may hold values from 1 to 2048, 81920 in all
- stiffness: float32 [4096, 32], P('win'), may hold values from 0.5 to 19
- centers: float32 [4096, 32], P('win'), may hold values from 0.1 to 3.7
Outputs:
- free_energy: float32 [4096], P('win')
Inputs may be any that keep to these rules, and one draw needn't show every extreme that they name: The frames of a block occupy its first slots; the lengths add up to 81920 and the largest is 2048. `sample_ids`: slots beyond a block's length hold ids that are not used; exactly 512 windows appear in no slot.
All inputs are finite; a program needn't handle non-finite values.
Results may differ from a plain program's by a relative error of at most 0.0003.
Values sent between devices are 32-bit elements; how exact they have to be, the bound alone decides.
No kernel may reach another device: no remote copies, remote signals or barrier semaphores. Data moves between devices by JAX's collectives and lax.ppermute only.
A program may use at most 64 MiB of HBM per device.

v0:
```python
import jax
import jax.numpy as jnp
from jax import lax
from jax.sharding import PartitionSpec as P

ITERS = 2
BAL = 1280
floor_value = -1e30


def coefficients(stiffness, centers):
    constant = jnp.sum(0.5 * stiffness * centers * centers, axis=1, keepdims=True)
    return jnp.concatenate([constant, -stiffness * centers, 0.5 * stiffness], axis=1)


def features(separations):
    unit_row = jnp.ones((1, separations.shape[1]), separations.dtype)
    return jnp.concatenate([unit_row, separations, separations * separations], axis=0)


def energies(coef_rows, separations):
    return jnp.dot(
        coef_rows,
        features(separations),
        precision=lax.Precision.HIGHEST,
        preferred_element_type=jnp.float32,
    )


def pair_combine(earlier, latter):
    top_all = jnp.maximum(earlier[0], latter[0])
    merged = earlier[1] * jnp.exp(earlier[0] - top_all) + latter[1] * jnp.exp(latter[0] - top_all)
    return (top_all, merged)


def pick_block(slot_total):
    return 512 if slot_total % 512 == 0 else slot_total


def denominators(highest, summed):
    global_top = lax.pmax(highest, "win")
    summed = lax.psum(summed * jnp.exp(highest - global_top), "win")
    highest = global_top
    return highest + jnp.log(summed)


def window_totals(highest, summed):
    global_top = lax.pmax(highest, "frame")
    summed = lax.psum(summed * jnp.exp(highest - global_top), "frame")
    highest = global_top
    return -(highest + jnp.log(summed))


def on_device(distances, sample_ids, lengths, stiffness, centers):
    coef_rows = coefficients(stiffness, centers)
    local_windows = stiffness.shape[0]
    restraints, capacity = distances.shape
    my_index = lax.axis_index("frame")
    own_length = lax.dynamic_index_in_dim(lengths, my_index, keepdims=False)
    slot_index = jnp.arange(capacity, dtype=jnp.int32)
    slot_usable = slot_index < own_length
    numbers = lax.axis_index("win") * local_windows + jnp.arange(local_windows, dtype=jnp.int32)
    count_len = pick_block(capacity)
    id_blocks = sample_ids.reshape(capacity // count_len, count_len)
    use_blocks = slot_usable.reshape(capacity // count_len, count_len)

    def count_block(running, inputs):
        id_block, use_block = inputs
        matches = (id_block[None, :] == numbers[:, None]) & use_block[None, :]
        return (running + jnp.sum(matches.astype(jnp.float32), axis=1), None)

    local_counts, _ = lax.scan(
        count_block, jnp.zeros((local_windows,), jnp.float32), (id_blocks, use_blocks)
    )
    counts = lax.psum(local_counts, "frame")
    frame_devices = lax.axis_size("frame")
    row_count = capacity // frame_devices
    offsets = jnp.cumsum(lengths) - lengths
    own_offset = lax.dynamic_index_in_dim(offsets, my_index, keepdims=False)
    arranged = distances.reshape(restraints, row_count, frame_devices)
    rolled = jnp.roll(arranged, own_offset % frame_devices, axis=2)
    received = lax.all_to_all(rolled, "frame", split_axis=2, concat_axis=2, tiled=True)
    lead_slot = (my_index - offsets) % frame_devices
    delivered = jnp.maximum((lengths - lead_slot + frame_devices - 1) // frame_devices, 0)
    begin_at = jnp.cumsum(delivered) - delivered
    target = jnp.arange(BAL, dtype=jnp.int32)
    source = jnp.sum(((begin_at + delivered)[None, :] <= target[:, None]).astype(jnp.int32), axis=1)
    within = target - jnp.take(begin_at, source)
    received_flat = received.reshape(restraints, row_count * frame_devices)
    frames_here = jnp.take(received_flat, within * frame_devices + source, axis=1)
    usable = jnp.ones((BAL,), jnp.bool_)
    sampled = counts > 0.5
    log_count = jnp.log(jnp.maximum(counts, 1.0))
    slot_total = frames_here.shape[1]
    block_len = pick_block(slot_total)
    block_count = slot_total // block_len
    frame_blocks = frames_here.reshape(restraints, block_count, block_len).transpose(1, 0, 2)
    usable_blocks = usable.reshape(block_count, block_len)
    free_energy = jnp.zeros((local_windows,), jnp.float32)
    for iteration in range(ITERS):
        shifted = log_count + free_energy

        def den_block(separations):
            energy = energies(coef_rows, separations)
            exponent = jnp.where(sampled[:, None], shifted[:, None] - energy, floor_value)
            highest = jnp.max(exponent, axis=0)
            summed = jnp.sum(
                jnp.where(sampled[:, None], jnp.exp(exponent - highest[None, :]), 0.0), axis=0
            )
            return (highest, summed)

        highest, summed = lax.map(den_block, frame_blocks)
        log_den = denominators(highest.reshape(-1), summed.reshape(-1)).reshape(
            block_count, block_len
        )

        def frame_block(running, inputs):
            separations, den_values, use_block = inputs
            energy = energies(coef_rows, separations)
            exponent = jnp.where(use_block[None, :], -energy - den_values[None, :], floor_value)
            block_top = jnp.max(exponent, axis=1)
            block_sum = jnp.sum(
                jnp.where(use_block[None, :], jnp.exp(exponent - block_top[:, None]), 0.0), axis=1
            )
            return (pair_combine(running, (block_top, block_sum)), None)

        start_value = (
            jnp.full((local_windows,), floor_value, jnp.float32),
            jnp.zeros((local_windows,), jnp.float32),
        )
        running, _ = lax.scan(frame_block, start_value, (frame_blocks, log_den, usable_blocks))
        free_energy = window_totals(running[0], running[1])
    return free_energy


def solution(mesh):
    return jax.shard_map(
        on_device,
        mesh=mesh,
        in_specs=(P(None, "frame"), P("frame"), P(), P("win", None), P("win", None)),
        out_specs=P("win"),
        check_vma=False,
    )
```

profile of v0, /device:TPU:2, one launch (start us, length us, event | category | flops | bytes accessed | tf_op | source)
XLA Modules:
  0.0 835.0 jit_solution(18027603402774270897)
XLA Ops:
  0.0 0.7 copy.18
  4.2 1.2 reshape.159
  5.8 0.9 copy.22
  6.7 1.2 reshape.445
  7.9 18.6 %all-to-all-start = ((f32[64,1,1024]{2,1,0:T(1,128)}), f32[64,1,1024]{2,1,0:T(1,128)S(1)}, u32[]{:S(2)}, u32[]{:S(2)}) async-start(f32[64,1,1024]{2,1,0:T(1,128)} %reshape.445), calls=%async_computation | async-start | bytes 524288 | tf_op jit(solution)/shard_map/all_to_all | solution.py:82
  28.3 0.7 fusion.26
  29.0 0.7 fusion.25
  29.7 0.7 fusion.24
  31.1 1.6 while.3
  32.7 139.1 %psum.35 = f32[512]{0:T(512)S(1)} all-reduce(f32[512]{0:T(512)S(1)} %get-tuple-element.89), channel_id=1, replica_groups=mesh['win'=8,'frame'=64] {'frame'}, use_global_device_ids=true, to_apply=%region_7.8 | all-reduce | flops 512 | bytes 4096 | tf_op jit(solution)/shard_map/psum | solution.py:75
  171.8 4.4 fusion.16
  176.2 0.9 compare_reduce_fusion.56
  177.2 35.6 %compare_and_fusion = (pred[1280]{0:T(1024)(128)(4,1)S(1)}, s32[1280]{0:T(1024)S(1)}) fusion(s32[1280]{0:T(1024)S(1)} %convert_reduce_fusion.1, pred[1280]{0:T(1024)(128)(4,1)S(1)} %get-tuple-element.188, pred[1280]{0:T(1024)(128)(4,1)S(1)} %get-tuple-element.186, pred[1280]{0:T(1024)(128)(4,1)S(1)} %get-tuple-element.187, ...), kind=kLoop, calls=%fused_computation.111 | loop fusion | flops 93440 | bytes 89828 | tf_op jit(solution)/shard_map/jit(_take)/and | solution.py:90
  213.5 1.3 reduce.122
  215.7 2.4 gather_fusion
  218.3 2.9 fusion.2
  221.2 12.7 %pmax.28 = f32[1280]{0:T(1024)S(1)} all-reduce(f32[1280]{0:T(1024)S(1)} %get-tuple-element.274), channel_id=1, replica_groups=mesh['win'=8,'frame'=64] {'win'}, use_global_device_ids=true, to_apply=%region_9.10 | all-reduce | flops 1280 | bytes 10240 | tf_op jit(solution)/shard_map/pmax | solution.py:41
  234.6 12.9 %psum.36 = f32[1280]{0:T(1024)S(1)} all-reduce(f32[1280]{0:T(1024)S(1)} %exponential_multiply_fusion.1), channel_id=1, replica_groups=mesh['win'=8,'frame'=64] {'win'}, use_global_device_ids=true, to_apply=%region_11.12 | all-reduce | flops 1280 | bytes 10240 | tf_op jit(solution)/shard_map/psum | solution.py:42
  248.5 142.5 %pmax.29 = f32[512]{0:T(512)S(1)} all-reduce(f32[512]{0:T(512)S(1)} %broadcast_maximum_fusion.1), channel_id=1, replica_groups=mesh['win'=8,'frame'=64] {'frame'}, use_global_device_ids=true, to_apply=%region_13.14 | all-reduce | flops 512 | bytes 4096 | tf_op jit(solution)/shard_map/pmax | solution.py:48
  391.0 138.0 %psum.37 = f32[512]{0:T(512)S(1)} all-reduce(f32[512]{0:T(512)S(1)} %exponential_multiply_fusion.3), channel_id=1, replica_groups=mesh['win'=8,'frame'=64] {'frame'}, use_global_device_ids=true, to_apply=%region_15.16 | all-reduce | flops 512 | bytes 4096 | tf_op jit(solution)/shard_map/psum | solution.py:49
  530.0 12.7 %pmax.30 = f32[1280]{0:T(1024)S(1)} all-reduce(f32[1280]{0:T(1024)S(1)} %fusion.3), channel_id=1, replica_groups=mesh['win'=8,'frame'=64] {'win'}, use_global_device_ids=true, to_apply=%region_17.18 | all-reduce | flops 1280 | bytes 10240 | tf_op jit(solution)/shard_map/pmax | solution.py:41
  542.7 12.7 %psum.38 = f32[1280]{0:T(1024)S(1)} all-reduce(f32[1280]{0:T(1024)S(1)} %exponential_multiply_fusion), channel_id=1, replica_groups=mesh['win'=8,'frame'=64] {'win'}, use_global_device_ids=true, to_apply=%region_19.20 | all-reduce | flops 1280 | bytes 10240 | tf_op jit(solution)/shard_map/psum | solution.py:42
  556.4 140.0 %pmax.31 = f32[512]{0:T(512)S(1)} all-reduce(f32[512]{0:T(512)S(1)} %broadcast_maximum_fusion), channel_id=1, replica_groups=mesh['win'=8,'frame'=64] {'frame'}, use_global_device_ids=true, to_apply=%region_21.22 | all-reduce | flops 512 | bytes 4096 | tf_op jit(solution)/shard_map/pmax | solution.py:48
  696.4 138.0 %psum.39 = f32[512]{0:T(512)S(1)} all-reduce(f32[512]{0:T(512)S(1)} %exponential_multiply_fusion.2), channel_id=1, replica_groups=mesh['win'=8,'frame'=64] {'frame'}, use_global_device_ids=true, to_apply=%region_23.24 | all-reduce | flops 512 | bytes 4096 | tf_op jit(solution)/shard_map/psum | solution.py:49
  (71 shorter events, 11.8 us)
Async XLA Ops:
  4.2 22.3 %copy-start.3 = (s32[64]{0:T(128)S(1)}, s32[64]{0:T(128)}, u32[]{:S(2)}) copy-start(s32[64]{0:T(128)} %param.9) | copy-start | bytes 772
  4.2 26.9 %copy-start.2 = (s32[2048]{0:T(1024)S(1)}, s32[2048]{0:T(1024)}, u32[]{:S(2)}) copy-start(s32[2048]{0:T(1024)} %param.8) | copy-start | bytes 24580
  5.4 207.5 %copy-start = (f32[512,32]{0,1:T(8,128)S(1)}, f32[512,32]{0,1:T(8,128)}, u32[]{:S(2)}) copy-start(f32[512,32]{0,1:T(8,128)} %param.11) | copy-start | bytes 196612
  5.4 207.5 %copy-start.1 = (f32[512,32]{0,1:T(8,128)S(1)}, f32[512,32]{0,1:T(8,128)}, u32[]{:S(2)}) copy-start(f32[512,32]{0,1:T(8,128)} %param.10) | copy-start | bytes 196612
  7.9 205.1 %all-to-all-start = ((f32[64,1,1024]{2,1,0:T(1,128)}), f32[64,1,1024]{2,1,0:T(1,128)S(1)}, u32[]{:S(2)}, u32[]{:S(2)}) async-start(f32[64,1,1024]{2,1,0:T(1,128)} %reshape.445), calls=%async_computation | async-start | bytes 524288 | tf_op jit(solution)/shard_map/all_to_all | solution.py:82
where the time goes:
time: 836 us; the launch traced here: 835 us
  blocking collectives  748 us (89%)
  other arithmetic  50.4 us (6%)
  starting transfers between devices  18.6 us (2%)
  local copies, waits for them, and re-layouts  12.1 us (1%)
    pmax x2, blocking collectives, window_totals(): global_top = lax.pmax(highest, 'frame')  282 us
    psum x2, blocking collectives, window_totals(): summed = lax.psum(summed * jnp.exp(highest - global_top), 'frame')  276 us
    psum x1, blocking collectives, on_device(): counts = lax.psum(local_counts, 'frame')  139 us
    and x1, other arithmetic, on_device(): jnp.take(received_flat, within * frame_devices + source, axis=1)  35.6 us
    psum x2, blocking collectives, denominators(): summed = lax.psum(summed * jnp.exp(highest - global_top), 'win')  25.6 us
    pmax x2, blocking collectives, denominators(): global_top = lax.pmax(highest, 'win')  25.3 us
    all_to_all x1, starting transfers between devices, on_device(): lax.all_to_all(rolled, 'frame', split_axis=2, concat_axis=2, tiled=True)  18.6 us
  transfers between devices with their start and end apart: 1, of which 0 were waited for; matrix products, arithmetic and copies ran while one was open for 6% of the time, Pallas kernels for 0%

commit v1 on v0

--- a/solution.py
+++ b/solution.py
@@ -46,7 +46,7 @@
 
 def window_totals(highest, summed):
     global_top = lax.pmax(highest, "frame")
-    summed = lax.psum(summed * jnp.exp(highest - global_top), "frame")
+    summed = jnp.sum(lax.all_gather(summed * jnp.exp(highest - global_top), "frame"), axis=0)
     highest = global_top
     return -(highest + jnp.log(summed))
 

time: 836 us -> 755 us (0.903)
  blocking collectives: 748 us -> 668 us
    psum x2 -> x0, blocking collectives: 276 us -> none  [window_totals(): summed = lax.psum(summed * jnp.exp(highest - global_top), 'frame')]
    all_gather x0 -> x2, blocking collectives: none -> 195 us  [window_totals(): lax.all_gather(summed * jnp.exp(highest - global_top), 'frame')]
where the time goes in v1:
time: 755 us; the launch traced here: 754 us
  blocking collectives  668 us (88%)
  other arithmetic  50.7 us (7%)
  starting transfers between devices  18.6 us (2%)
  local copies, waits for them, and re-layouts  12.1 us (2%)
    pmax x2, blocking collectives, window_totals(): global_top = lax.pmax(highest, 'frame')  282 us
    all_gather x2, blocking collectives, window_totals(): lax.all_gather(summed * jnp.exp(highest - global_top), 'frame')  195 us
    psum x1, blocking collectives, on_device(): counts = lax.psum(local_counts, 'frame')  139 us
    and x1, other arithmetic, on_device(): jnp.take(received_flat, within * frame_devices + source, axis=1)  35.6 us
    psum x2, blocking collectives, denominators(): summed = lax.psum(summed * jnp.exp(highest - global_top), 'win')  25.6 us
    pmax x2, blocking collectives, denominators(): global_top = lax.pmax(highest, 'win')  25.3 us
    all_to_all x1, starting transfers between devices, on_device(): lax.all_to_all(rolled, 'frame', split_axis=2, concat_axis=2, tiled=True)  18.6 us
  transfers between devices with their start and end apart: 1, of which 0 were waited for; matrix products, arithmetic and copies ran while one was open for 6% of the time, Pallas kernels for 0%

profile of v1, /device:TPU:2, one launch (start us, length us, event | category | flops | bytes accessed | tf_op | source)
XLA Modules:
  0.0 754.3 jit_solution(914710049426218248)
XLA Ops:
  0.0 0.7 copy.18
  4.2 1.2 reshape.159
  5.8 0.9 copy.22
  6.7 1.2 reshape.453
  7.9 18.6 %all-to-all-start = ((f32[64,1,1024]{2,1,0:T(1,128)}), f32[64,1,1024]{2,1,0:T(1,128)S(1)}, u32[]{:S(2)}, u32[]{:S(2)}) async-start(f32[64,1,1024]{2,1,0:T(1,128)} %reshape.453), calls=%async_computation | async-start | bytes 524288 | tf_op jit(solution)/shard_map/all_to_all | solution.py:82
  28.3 0.7 fusion.26
  29.0 0.7 fusion.25
  29.7 0.7 fusion.24
  31.1 1.6 while.3
  32.7 139.1 %psum.21 = f32[512]{0:T(512)S(1)} all-reduce(f32[512]{0:T(512)S(1)} %get-tuple-element.89), channel_id=1, replica_groups=mesh['win'=8,'frame'=64] {'frame'}, use_global_device_ids=true, to_apply=%region_7.8 | all-reduce | flops 512 | bytes 4096 | tf_op jit(solution)/shard_map/psum | solution.py:75
  171.8 4.4 fusion.16
  176.2 0.9 compare_reduce_fusion.56
  177.2 35.6 %compare_and_fusion = (pred[1280]{0:T(1024)(128)(4,1)S(1)}, s32[1280]{0:T(1024)S(1)}) fusion(s32[1280]{0:T(1024)S(1)} %convert_reduce_fusion.1, pred[1280]{0:T(1024)(128)(4,1)S(1)} %get-tuple-element.188, pred[1280]{0:T(1024)(128)(4,1)S(1)} %get-tuple-element.186, pred[1280]{0:T(1024)(128)(4,1)S(1)} %get-tuple-element.187, ...), kind=kLoop, calls=%fused_computation.111 | loop fusion | flops 93440 | bytes 89828 | tf_op jit(solution)/shard_map/jit(_take)/and | solution.py:90
  213.5 1.3 reduce.124
  215.7 2.4 gather_fusion
  218.3 2.9 fusion.2
  221.2 12.7 %pmax.28 = f32[1280]{0:T(1024)S(1)} all-reduce(f32[1280]{0:T(1024)S(1)} %get-tuple-element.274), channel_id=1, replica_groups=mesh['win'=8,'frame'=64] {'win'}, use_global_device_ids=true, to_apply=%region_9.10 | all-reduce | flops 1280 | bytes 10240 | tf_op jit(solution)/shard_map/pmax | solution.py:41
  234.6 12.9 %psum.22 = f32[1280]{0:T(1024)S(1)} all-reduce(f32[1280]{0:T(1024)S(1)} %exponential_multiply_fusion.1), channel_id=1, replica_groups=mesh['win'=8,'frame'=64] {'win'}, use_global_device_ids=true, to_apply=%region_11.12 | all-reduce | flops 1280 | bytes 10240 | tf_op jit(solution)/shard_map/psum | solution.py:42
  248.5 142.5 %pmax.29 = f32[512]{0:T(512)S(1)} all-reduce(f32[512]{0:T(512)S(1)} %broadcast_maximum_fusion.1), channel_id=1, replica_groups=mesh['win'=8,'frame'=64] {'frame'}, use_global_device_ids=true, to_apply=%region_13.14 | all-reduce | flops 512 | bytes 4096 | tf_op jit(solution)/shard_map/pmax | solution.py:48
  391.0 96.5 %all-gather.2 = f32[64,1,512]{2,1,0:T(1,128)S(1)} all-gather(f32[1,1,512]{2,1,0:T(1,128)S(1)} %bitcast.86), channel_id=2, replica_groups=mesh['win'=8,'frame'=64] {'frame'}, dimensions={0}, use_global_device_ids=true | all-gather | bytes 133120 | tf_op jit(solution)/shard_map/all_gather | solution.py:49
  488.6 12.7 %pmax.30 = f32[1280]{0:T(1024)S(1)} all-reduce(f32[1280]{0:T(1024)S(1)} %fusion.3), channel_id=1, replica_groups=mesh['win'=8,'frame'=64] {'win'}, use_global_device_ids=true, to_apply=%region_17.18 | all-reduce | flops 1280 | bytes 10240 | tf_op jit(solution)/shard_map/pmax | solution.py:41
  501.3 12.7 %psum.23 = f32[1280]{0:T(1024)S(1)} all-reduce(f32[1280]{0:T(1024)S(1)} %exponential_multiply_fusion), channel_id=1, replica_groups=mesh['win'=8,'frame'=64] {'win'}, use_global_device_ids=true, to_apply=%region_19.20 | all-reduce | flops 1280 | bytes 10240 | tf_op jit(solution)/shard_map/psum | solution.py:42
  515.0 140.0 %pmax.31 = f32[512]{0:T(512)S(1)} all-reduce(f32[512]{0:T(512)S(1)} %broadcast_maximum_fusion), channel_id=1, replica_groups=mesh['win'=8,'frame'=64] {'frame'}, use_global_device_ids=true, to_apply=%region_21.22 | all-reduce | flops 512 | bytes 4096 | tf_op jit(solution)/shard_map/pmax | solution.py:48
  655.0 98.6 %all-gather.3 = f32[64,1,512]{2,1,0:T(1,128)S(1)} all-gather(f32[1,1,512]{2,1,0:T(1,128)S(1)} %bitcast.87), channel_id=3, replica_groups=mesh['win'=8,'frame'=64] {'frame'}, dimensions={0}, use_global_device_ids=true | all-gather | bytes 133120 | tf_op jit(solution)/shard_map/all_gather | solution.py:49
  (73 shorter events, 12.1 us)
Async XLA Ops:
  4.2 22.3 %copy-start.3 = (s32[64]{0:T(128)S(1)}, s32[64]{0:T(128)}, u32[]{:S(2)}) copy-start(s32[64]{0:T(128)} %param.9) | copy-start | bytes 772
  4.2 26.9 %copy-start.2 = (s32[2048]{0:T(1024)S(1)}, s32[2048]{0:T(1024)}, u32[]{:S(2)}) copy-start(s32[2048]{0:T(1024)} %param.8) | copy-start | bytes 24580
  5.4 207.5 %copy-start = (f32[512,32]{0,1:T(8,128)S(1)}, f32[512,32]{0,1:T(8,128)}, u32[]{:S(2)}) copy-start(f32[512,32]{0,1:T(8,128)} %param.11) | copy-start | bytes 196612
  5.4 207.5 %copy-start.1 = (f32[512,32]{0,1:T(8,128)S(1)}, f32[512,32]{0,1:T(8,128)}, u32[]{:S(2)}) copy-start(f32[512,32]{0,1:T(8,128)} %param.10) | copy-start | bytes 196612
  7.9 205.1 %all-to-all-start = ((f32[64,1,1024]{2,1,0:T(1,128)}), f32[64,1,1024]{2,1,0:T(1,128)S(1)}, u32[]{:S(2)}, u32[]{:S(2)}) async-start(f32[64,1,1024]{2,1,0:T(1,128)} %reshape.453), calls=%async_computation | async-start | bytes 524288 | tf_op jit(solution)/shard_map/all_to_all | solution.py:82
